TPU v7x, 32 devices: a whole 2x2x4 slice. The times are simulated.
32 devices in a mesh: shard: 4 (over y, x), rep: 8 (over z, core).
Axes of the slice: x: 2, y: 2, z: 4, core: 2. Of those that a mesh axis runs over, the one named last changes fastest.
Arguments:
- latents: bfloat16 [32, 256, 384], P(('shard', 'rep')), may hold values from -6 to 6
- condition: bfloat16 [32, 384], P(('shard', 'rep')), may hold values from -4 to 4
- cotangent: bfloat16 [32, 256, 384], P(('shard', 'rep')), may hold values from -6 to 6
- w_qkv: bfloat16 [2, 384, 1152], P(None, 'shard'), may hold values from -0.15625 to 0.15625
- b_qv: bfloat16 [2, 768], P(None, 'shard'), may hold values from -3 to 3
- w_proj: bfloat16 [2, 384, 384], P(None, 'shard'), may hold values from -1.75 to 1.75
- b_proj: bfloat16 [2, 384], P(None, 'shard'), may hold values from -3 to 3
- w_fc1: bfloat16 [2, 384, 1536], P(None, 'shard'), may hold values from -0.3125 to 0.3125
- b_fc1: bfloat16 [2, 1536], P(None, 'shard'), may hold values from -3 to 3
- w_fc2: bfloat16 [2, 1536, 384], P(None, 'shard'), may hold values from -0.15625 to 0.15625
- b_fc2: bfloat16 [2, 384], P(None, 'shard'), may hold values from -3 to 3
- w_ada: bfloat16 [2, 384, 2304], P(None, 'shard'), may hold values from -4 to 4
- b_ada: bfloat16 [2, 2304], P(None, 'shard'), may hold values from -3 to 3
Outputs:
- x_out: bfloat16 [32, 256, 384], P(('shard', 'rep'))
- x_grad: float32 [32, 256, 384], P(('shard', 'rep'))
- cond_grad: float32 [32, 384], P(('shard', 'rep'))
- grad_qkv: float32 [2, 384, 1152], P(None, 'shard')
- grad_qv_bias: float32 [2, 768], P(None, 'shard')
- grad_proj: float32 [2, 384, 384], P(None, 'shard')
- grad_proj_bias: float32 [2, 384], P(None, 'shard')
- grad_fc1: float32 [2, 384, 1536], P(None, 'shard')
- grad_fc1_bias: float32 [2, 1536], P(None, 'shard')
- grad_fc2: float32 [2, 1536, 384], P(None, 'shard')
- grad_fc2_bias: float32 [2, 384], P(None, 'shard')
- grad_ada: float32 [2, 384, 2304], P(None, 'shard')
- grad_ada_bias: float32 [2, 2304], P(None, 'shard')
All inputs are finite; a program needn't handle non-finite values.
Results may differ from a plain program's by a relative error of at most 0.017.
Values may be sent and summed in bfloat16 or wider, within the bound.
No kernel may reach another device: no remote copies, remote signals or barrier semaphores. Data moves between devices by JAX's collectives and lax.ppermute only.
A program may use at most 128 MiB of HBM per device.

v0:
```python
import jax
import jax.numpy as jnp
from jax import lax
from jax.sharding import PartitionSpec as P

HEADS = 6


def layer_norm(residual_state):
    center = residual_state - jnp.mean(residual_state, axis=-1, keepdims=True)
    inverse = lax.rsqrt(jnp.mean(center * center, axis=-1, keepdims=True) + 1e-06)
    return (center * inverse, inverse)


def norm_back(grad_norm, normed, inverse):
    centered = grad_norm - jnp.mean(grad_norm, axis=-1, keepdims=True)
    return inverse * (centered - normed * jnp.mean(grad_norm * normed, axis=-1, keepdims=True))


def project(left, right):
    return jnp.einsum("lsd,de->lse", left, right, preferred_element_type=jnp.float32)


def project_back(left, right):
    return jnp.einsum("lse,de->lsd", left, right, preferred_element_type=jnp.float32)


def weight_grad(left, right):
    return jnp.einsum("lsd,lse->de", left, right, preferred_element_type=jnp.float32)


def column_sums(grad_low):
    return jnp.sum(grad_low.astype(jnp.float32), axis=(0, 1))


def split_heads(tensor):
    return tensor.reshape(tensor.shape[0], tensor.shape[1], HEADS, tensor.shape[2] // HEADS)


def forward_layer(gathered, residual_state, condition_activation):
    w_qkv, b_qv, w_proj, b_proj, w_fc1, b_fc1, w_fc2, b_fc2, w_ada, b_ada = gathered
    width = residual_state.shape[2]
    modulate = jnp.dot(
        condition_activation, w_ada, preferred_element_type=jnp.float32
    ) + b_ada.astype(jnp.float32)
    pieces = [part_mod[:, None, :] for part_mod in jnp.split(modulate, 6, axis=-1)]
    shift_one, scale_one, gate_one, shift_two, scale_two, gate_two = pieces
    normed_one, inverse_one = layer_norm(residual_state)
    h_one = (normed_one * (1.0 + scale_one) + shift_one).astype(jnp.bfloat16)
    mixed = project(h_one, w_qkv)
    bias_wide = b_qv.astype(jnp.float32)
    queries = split_heads((mixed[..., :width] + bias_wide[:width]).astype(jnp.bfloat16))
    key_rows = split_heads(mixed[..., width : 2 * width].astype(jnp.bfloat16))
    value_rows = split_heads((mixed[..., 2 * width :] + bias_wide[width:]).astype(jnp.bfloat16))
    scale_dot = (width // HEADS) ** (-0.5)
    scores = (
        jnp.einsum("lqhd,lkhd->lhqk", queries, key_rows, preferred_element_type=jnp.float32)
        * scale_dot
    )
    top_score = jnp.max(scores, axis=-1, keepdims=True)
    log_total = top_score + jnp.log(jnp.sum(jnp.exp(scores - top_score), axis=-1, keepdims=True))
    probs_low = jnp.exp(scores - log_total).astype(jnp.bfloat16)
    attended = jnp.einsum(
        "lhqk,lkhd->lqhd", probs_low, value_rows, preferred_element_type=jnp.float32
    )
    attended = attended.reshape(residual_state.shape).astype(jnp.bfloat16)
    branch = project(attended, w_proj) + b_proj.astype(jnp.float32)
    middle = residual_state + gate_one * branch
    normed_two, inverse_two = layer_norm(middle)
    h_two = (normed_two * (1.0 + scale_two) + shift_two).astype(jnp.bfloat16)
    pre_act = project(h_two, w_fc1) + b_fc1.astype(jnp.float32)
    act_low = jax.nn.gelu(pre_act, approximate=True).astype(jnp.bfloat16)
    mlp_out = project(act_low, w_fc2) + b_fc2.astype(jnp.float32)
    stream_next = middle + gate_two * mlp_out
    stored = (
        pieces,
        normed_one,
        inverse_one,
        h_one,
        queries,
        key_rows,
        value_rows,
        log_total,
        attended,
        branch,
        normed_two,
        inverse_two,
        h_two,
        pre_act,
        act_low,
        mlp_out,
    )
    return (stream_next, stored)


def backward_layer(gathered, stored, grad_out, condition_activation):
    w_qkv, b_qv, w_proj, b_proj, w_fc1, b_fc1, w_fc2, b_fc2, w_ada, b_ada = gathered
    (
        pieces,
        normed_one,
        inverse_one,
        h_one,
        queries,
        key_rows,
        value_rows,
        log_total,
        attended,
        branch,
        normed_two,
        inverse_two,
        h_two,
        pre_act,
        act_low,
        mlp_out,
    ) = stored
    shift_one, scale_one, gate_one, shift_two, scale_two, gate_two = pieces
    width = grad_out.shape[2]
    scale_dot = (width // HEADS) ** (-0.5)
    d_gate_two = jnp.sum(grad_out * mlp_out, axis=1)
    d_mlp = (grad_out * gate_two).astype(jnp.bfloat16)
    g_fc2 = weight_grad(act_low, d_mlp)
    gb_fc2 = column_sums(d_mlp)
    d_act = project_back(d_mlp, w_fc2)
    gelu_pull = jax.vjp(lambda pre_in: jax.nn.gelu(pre_in, approximate=True), pre_act)[1]
    d_pre = gelu_pull(d_act)[0].astype(jnp.bfloat16)
    g_fc1 = weight_grad(h_two, d_pre)
    gb_fc1 = column_sums(d_pre)
    d_h_two = project_back(d_pre, w_fc1)
    d_shift_two = jnp.sum(d_h_two, axis=1)
    d_scale_two = jnp.sum(d_h_two * normed_two, axis=1)
    d_middle = grad_out + norm_back(d_h_two * (1.0 + scale_two), normed_two, inverse_two)
    d_gate_one = jnp.sum(d_middle * branch, axis=1)
    d_branch = (d_middle * gate_one).astype(jnp.bfloat16)
    g_proj = weight_grad(attended, d_branch)
    gb_proj = column_sums(d_branch)
    d_attended = split_heads(project_back(d_branch, w_proj).astype(jnp.bfloat16))
    scores = (
        jnp.einsum("lqhd,lkhd->lhqk", queries, key_rows, preferred_element_type=jnp.float32)
        * scale_dot
    )
    probs = jnp.exp(scores - log_total)
    probs_low = probs.astype(jnp.bfloat16)
    d_values = jnp.einsum(
        "lhqk,lqhd->lkhd", probs_low, d_attended, preferred_element_type=jnp.float32
    )
    d_probs = jnp.einsum(
        "lqhd,lkhd->lhqk", d_attended, value_rows, preferred_element_type=jnp.float32
    )
    d_scores = (probs * (d_probs - jnp.sum(probs * d_probs, axis=-1, keepdims=True))).astype(
        jnp.bfloat16
    )
    d_queries = (
        jnp.einsum("lhqk,lkhd->lqhd", d_scores, key_rows, preferred_element_type=jnp.float32)
        * scale_dot
    )
    d_keys = (
        jnp.einsum("lhqk,lqhd->lkhd", d_scores, queries, preferred_element_type=jnp.float32)
        * scale_dot
    )
    flat_shape = grad_out.shape
    d_qkv = jnp.concatenate(
        [d_queries.reshape(flat_shape), d_keys.reshape(flat_shape), d_values.reshape(flat_shape)],
        axis=-1,
    ).astype(jnp.bfloat16)
    g_qkv = weight_grad(h_one, d_qkv)
    qkv_sums = column_sums(d_qkv)
    gb_qv = jnp.concatenate([qkv_sums[:width], qkv_sums[2 * width :]])
    d_h_one = project_back(d_qkv, w_qkv)
    d_shift_one = jnp.sum(d_h_one, axis=1)
    d_scale_one = jnp.sum(d_h_one * normed_one, axis=1)
    d_stream = d_middle + norm_back(d_h_one * (1.0 + scale_one), normed_one, inverse_one)
    d_mod = jnp.concatenate(
        [d_shift_one, d_scale_one, d_gate_one, d_shift_two, d_scale_two, d_gate_two], axis=-1
    ).astype(jnp.bfloat16)
    g_ada = jnp.einsum("ld,le->de", condition_activation, d_mod, preferred_element_type=jnp.float32)
    gb_ada = jnp.sum(d_mod.astype(jnp.float32), axis=0)
    d_cond = jnp.einsum("le,de->ld", d_mod, w_ada, preferred_element_type=jnp.float32)
    grads = (g_qkv, gb_qv, g_proj, gb_proj, g_fc1, gb_fc1, g_fc2, gb_fc2, g_ada, gb_ada)
    return (d_stream, d_cond, grads)


def shards(
    latents,
    condition,
    cotangent,
    w_qkv,
    b_qv,
    w_proj,
    b_proj,
    w_fc1,
    b_fc1,
    w_fc2,
    b_fc2,
    w_ada,
    b_ada,
):
    layers = w_qkv.shape[0]
    total_latents = latents.shape[0] * lax.axis_size("shard") * lax.axis_size("rep")
    cond_in = condition.astype(jnp.float32)
    condition_activation = jax.nn.silu(cond_in).astype(jnp.bfloat16)
    residual_state = latents.astype(jnp.float32)
    gathered_all = []
    stored_all = []
    for layer_number in range(layers):
        gathered = (
            lax.all_gather(w_qkv[layer_number], "shard", axis=0, tiled=True),
            lax.all_gather(b_qv[layer_number], "shard", axis=0, tiled=True),
            lax.all_gather(w_proj[layer_number], "shard", axis=0, tiled=True),
            lax.all_gather(b_proj[layer_number], "shard", axis=0, tiled=True),
            lax.all_gather(w_fc1[layer_number], "shard", axis=0, tiled=True),
            lax.all_gather(b_fc1[layer_number], "shard", axis=0, tiled=True),
            lax.all_gather(w_fc2[layer_number], "shard", axis=0, tiled=True),
            lax.all_gather(b_fc2[layer_number], "shard", axis=0, tiled=True),
            lax.all_gather(w_ada[layer_number], "shard", axis=0, tiled=True),
            lax.all_gather(b_ada[layer_number], "shard", axis=0, tiled=True),
        )
        residual_state, stored = forward_layer(gathered, residual_state, condition_activation)
        gathered_all.append(gathered)
        stored_all.append(stored)
    x_out = residual_state.astype(jnp.bfloat16)
    grad_stream = cotangent.astype(jnp.float32)
    grad_cond = jnp.zeros(cond_in.shape, jnp.float32)
    collected = []
    for layer_number in reversed(range(layers)):
        gathered = (
            lax.all_gather(w_qkv[layer_number], "shard", axis=0, tiled=True),
            lax.all_gather(b_qv[layer_number], "shard", axis=0, tiled=True),
            lax.all_gather(w_proj[layer_number], "shard", axis=0, tiled=True),
            lax.all_gather(b_proj[layer_number], "shard", axis=0, tiled=True),
            lax.all_gather(w_fc1[layer_number], "shard", axis=0, tiled=True),
            lax.all_gather(b_fc1[layer_number], "shard", axis=0, tiled=True),
            lax.all_gather(w_fc2[layer_number], "shard", axis=0, tiled=True),
            lax.all_gather(b_fc2[layer_number], "shard", axis=0, tiled=True),
            lax.all_gather(w_ada[layer_number], "shard", axis=0, tiled=True),
            lax.all_gather(b_ada[layer_number], "shard", axis=0, tiled=True),
        )
        grad_stream, d_cond, grads = backward_layer(
            gathered, stored_all[layer_number], grad_stream, condition_activation
        )
        grad_cond = grad_cond + d_cond
        owner_rows = (
            lax.psum_scatter(
                grads[0].astype(jnp.bfloat16), "shard", scatter_dimension=0, tiled=True
            ).astype(jnp.float32),
            lax.psum_scatter(
                grads[1].astype(jnp.bfloat16), "shard", scatter_dimension=0, tiled=True
            ).astype(jnp.float32),
            lax.psum_scatter(
                grads[2].astype(jnp.bfloat16), "shard", scatter_dimension=0, tiled=True
            ).astype(jnp.float32),
            lax.psum_scatter(
                grads[3].astype(jnp.bfloat16), "shard", scatter_dimension=0, tiled=True
            ).astype(jnp.float32),
            lax.psum_scatter(
                grads[4].astype(jnp.bfloat16), "shard", scatter_dimension=0, tiled=True
            ).astype(jnp.float32),
            lax.psum_scatter(
                grads[5].astype(jnp.bfloat16), "shard", scatter_dimension=0, tiled=True
            ).astype(jnp.float32),
            lax.psum_scatter(
                grads[6].astype(jnp.bfloat16), "shard", scatter_dimension=0, tiled=True
            ).astype(jnp.float32),
            lax.psum_scatter(
                grads[7].astype(jnp.bfloat16), "shard", scatter_dimension=0, tiled=True
            ).astype(jnp.float32),
            lax.psum_scatter(
                grads[8].astype(jnp.bfloat16), "shard", scatter_dimension=0, tiled=True
            ).astype(jnp.float32),
            lax.psum_scatter(
                grads[9].astype(jnp.bfloat16), "shard", scatter_dimension=0, tiled=True
            ).astype(jnp.float32),
        )
        owner_rows = (
            lax.psum(owner_rows[0].astype(jnp.bfloat16), "rep").astype(jnp.float32),
            lax.psum(owner_rows[1].astype(jnp.bfloat16), "rep").astype(jnp.float32),
            lax.psum(owner_rows[2].astype(jnp.bfloat16), "rep").astype(jnp.float32),
            lax.psum(owner_rows[3].astype(jnp.bfloat16), "rep").astype(jnp.float32),
            lax.psum(owner_rows[4].astype(jnp.bfloat16), "rep").astype(jnp.float32),
            lax.psum(owner_rows[5].astype(jnp.bfloat16), "rep").astype(jnp.float32),
            lax.psum(owner_rows[6].astype(jnp.bfloat16), "rep").astype(jnp.float32),
            lax.psum(owner_rows[7].astype(jnp.bfloat16), "rep").astype(jnp.float32),
            lax.psum(owner_rows[8].astype(jnp.bfloat16), "rep").astype(jnp.float32),
            lax.psum(owner_rows[9].astype(jnp.bfloat16), "rep").astype(jnp.float32),
        )
        collected.insert(0, owner_rows)
    stacked = [
        jnp.stack([layer_rows[slot_no] for layer_rows in collected]) for slot_no in range(10)
    ]
    silu_pull = jax.vjp(jax.nn.silu, cond_in)[1]
    cond_grad = silu_pull(grad_cond)[0]
    inverse_count = 1.0 / total_latents
    return (
        x_out,
        grad_stream,
        cond_grad,
        stacked[0] * inverse_count,
        stacked[1] * inverse_count,
        stacked[2] * inverse_count,
        stacked[3] * inverse_count,
        stacked[4] * inverse_count,
        stacked[5] * inverse_count,
        stacked[6] * inverse_count,
        stacked[7] * inverse_count,
        stacked[8] * inverse_count,
        stacked[9] * inverse_count,
    )


def solution(mesh):
    return jax.shard_map(
        shards,
        mesh=mesh,
        in_specs=(
            P(("shard", "rep"), None, None),
            P(("shard", "rep"), None),
            P(("shard", "rep"), None, None),
            P(None, "shard", None),
            P(None, "shard"),
            P(None, "shard", None),
            P(None, "shard"),
            P(None, "shard", None),
            P(None, "shard"),
            P(None, "shard", None),
            P(None, "shard"),
            P(None, "shard", None),
            P(None, "shard"),
        ),
        out_specs=(
            P(("shard", "rep"), None, None),
            P(("shard", "rep"), None, None),
            P(("shard", "rep"), None),
            P(None, "shard", None),
            P(None, "shard"),
            P(None, "shard", None),
            P(None, "shard"),
            P(None, "shard", None),
            P(None, "shard"),
            P(None, "shard", None),
            P(None, "shard"),
            P(None, "shard", None),
            P(None, "shard"),
        ),
        check_vma=False,
    )
```

profile of v0, /device:TPU:0, one launch (start us, length us, event | category | flops | bytes accessed | tf_op | source)
XLA Modules:
  0.0 625.9 jit_solution(534134971308301505)
XLA Ops:
  17.0 9.5 %all-gather.17 = bf16[1,1536]{1,0:T(2,128)(2,1)S(1)} all-gather(bf16[1,384]{1,0:T(2,128)(2,1)S(1)} %get-tuple-element.131), channel_id=19, replica_groups=mesh['shard'=4,'rep'=8] {'shard'}, dimensions={1}, use_global_device_ids=true | all-gather | bytes 3840 | tf_op jit(solution)/shard_map/all_gather | solution.py:211
  27.2 8.0 %all-gather.7 = bf16[1,1536]{1,0:T(2,128)(2,1)S(1)} all-gather(bf16[1,384]{1,0:T(2,128)(2,1)S(1)} %get-tuple-element.132), channel_id=9, replica_groups=mesh['shard'=4,'rep'=8] {'shard'}, dimensions={1}, use_global_device_ids=true | all-gather | bytes 3840 | tf_op jit(solution)/shard_map/all_gather | solution.py:211
  37.5 15.8 %all-reduce.21 = (bf16[2304]{0:T(1024)(128)(2,1)S(1)}, bf16[768]{0:T(1024)(128)(2,1)S(1)}, bf16[384]{0:T(512)(128)(2,1)S(1)}, bf16[384]{0:T(512)(128)(2,1)S(1)},...) all-reduce(bf16[2304]{0:T(1024)(128)(2,1)S(1)} %dynamic-update-slic, ...), channel_id=3, replica_groups=mesh['shard'=4,'rep'=8] {'shard'}, use_global_device_ids=true, to_apply=%add | all-reduce | flops 7680 | bytes 30720
  56.3 10.3 %all-gather.14 = bf16[1,384,384]{2,1,0:T(8,128)(2,1)} all-gather(bf16[1,96,384]{2,1,0:T(8,128)(2,1)S(1)} %get-tuple-element.123), channel_id=16, replica_groups=mesh['shard'=4,'rep'=8] {'shard'}, dimensions={1}, use_global_device_ids=true | all-gather | bytes 368640 | tf_op jit(solution)/shard_map/all_gather | solution.py:208
  66.6 11.1 %all-gather.4 = bf16[1,384,384]{2,1,0:T(8,128)(2,1)S(1)} all-gather(bf16[1,96,384]{2,1,0:T(8,128)(2,1)S(1)} %get-tuple-element.124), channel_id=6, replica_groups=mesh['shard'=4,'rep'=8] {'shard'}, dimensions={1}, use_global_device_ids=true | all-gather | bytes 368640 | tf_op jit(solution)/shard_map/all_gather | solution.py:208
  77.7 14.5 %all-gather.12 = bf16[1,384,1152]{2,1,0:T(8,128)(2,1)S(1)} all-gather(bf16[1,96,1152]{2,1,0:T(8,128)(2,1)S(1)} %get-tuple-element.114), channel_id=14, replica_groups=mesh['shard'=4,'rep'=8] {'shard'}, dimensions={1}, use_global_device_ids=true | all-gather | bytes 1105920 | tf_op jit(solution)/shard_map/all_gather | solution.py:206
  92.2 14.5 %all-gather.2 = bf16[1,384,1152]{2,1,0:T(8,128)(2,1)S(1)} all-gather(bf16[1,96,1152]{2,1,0:T(8,128)(2,1)S(1)} %get-tuple-element.115), channel_id=4, replica_groups=mesh['shard'=4,'rep'=8] {'shard'}, dimensions={1}, use_global_device_ids=true | all-gather | bytes 1105920 | tf_op jit(solution)/shard_map/all_gather | solution.py:206
  115.7 4.5 all-gather.29.cloned.1.call-done
  123.2 26.4 %all-gather.31.cloned.1.call-done = bf16[1,1536,384]{2,1,0:T(8,128)(2,1)} async-done(((bf16[1,384,384]{2,1,0:T(8,128)(2,1)}), bf16[1,1536,384]{2,1,0:T(8,128)(2,1)}) %all-gather.31.cloned.1.call-update) | async-done | bytes 1179664 | tf_op jit(solution)/shard_map/all_gather | solution.py:212
  161.5 17.6 %all-gather.35.cloned.1.call-done = bf16[1,384,1536]{2,1,0:T(8,128)(2,1)} async-done(((bf16[1,96,1536]{2,1,0:T(8,128)(2,1)}), bf16[1,384,1536]{2,1,0:T(8,128)(2,1)}) %all-gather.35.cloned.1.call-update) | async-done | bytes 1179664 | tf_op jit(solution)/shard_map/all_gather | solution.py:210
  182.2 26.9 %all-gather.37.cloned.1.call-done = bf16[1,1536,384]{2,1,0:T(8,128)(2,1)} async-done(((bf16[1,384,384]{2,1,0:T(8,128)(2,1)}), bf16[1,1536,384]{2,1,0:T(8,128)(2,1)}) %all-gather.37.cloned.1.call-update) | async-done | bytes 1179664 | tf_op jit(solution)/shard_map/all_gather | solution.py:212
  209.1 4.0 fusion.165
  246.9 3.3 convolution_convert_fusion.2
  278.0 30.3 %reduce-scatter.13.cloned.1.call-done = bf16[96,1152]{1,0:T(8,128)(2,1)} async-done(((bf16[384,1152]{1,0:T(8,128)(2,1)}), bf16[96,1152]{1,0:T(8,128)(2,1)}) %reduce-scatter.13.cloned.1.call-update) | async-done | bytes 221200 | tf_op jit(solution)/shard_map/reduce_scatter | solution.py:242
  308.3 29.5 %reduce-scatter.11.cloned.1.call-done = bf16[96,1152]{1,0:T(8,128)(2,1)} async-done(((bf16[384,1152]{1,0:T(8,128)(2,1)}), bf16[96,1152]{1,0:T(8,128)(2,1)}) %reduce-scatter.11.cloned.1.call-update) | async-done | bytes 221200 | tf_op jit(solution)/shard_map/reduce_scatter | solution.py:242
  337.8 31.5 %reduce-scatter.25.cloned.1.call-done = bf16[384,384]{1,0:T(8,128)(2,1)} async-done(((bf16[1536,384]{1,0:T(8,128)(2,1)}), bf16[384,384]{1,0:T(8,128)(2,1)}) %reduce-scatter.25.cloned.1.call-update) | async-done | bytes 294928 | tf_op jit(solution)/shard_map/reduce_scatter | solution.py:260
  369.3 31.9 %reduce-scatter.21.cloned.1.call-done = bf16[96,1536]{1,0:T(8,128)(2,1)} async-done(((bf16[384,1536]{1,0:T(8,128)(2,1)}), bf16[96,1536]{1,0:T(8,128)(2,1)}) %reduce-scatter.21.cloned.1.call-update) | async-done | bytes 294928 | tf_op jit(solution)/shard_map/reduce_scatter | solution.py:254
  401.2 31.5 %reduce-scatter.23.cloned.1.call-done = bf16[384,384]{1,0:T(8,128)(2,1)} async-done(((bf16[1536,384]{1,0:T(8,128)(2,1)}), bf16[384,384]{1,0:T(8,128)(2,1)}) %reduce-scatter.23.cloned.1.call-update) | async-done | bytes 294928 | tf_op jit(solution)/shard_map/reduce_scatter | solution.py:260
  432.7 31.9 %reduce-scatter.19.cloned.1.call-done = bf16[96,1536]{1,0:T(8,128)(2,1)} async-done(((bf16[384,1536]{1,0:T(8,128)(2,1)}), bf16[96,1536]{1,0:T(8,128)(2,1)}) %reduce-scatter.19.cloned.1.call-update) | async-done | bytes 294928 | tf_op jit(solution)/shard_map/reduce_scatter | solution.py:254
  464.6 36.0 %reduce-scatter.27.cloned.1.call-done = bf16[96,2304]{1,0:T(8,128)(2,1)} async-done(((bf16[384,2304]{1,0:T(8,128)(2,1)}), bf16[96,2304]{1,0:T(8,128)(2,1)}) %reduce-scatter.27.cloned.1.call-update) | async-done | bytes 442384 | tf_op jit(solution)/shard_map/reduce_scatter | solution.py:266
  500.6 35.4 %reduce-scatter.29.cloned.1.call-done = bf16[96,2304]{1,0:T(8,128)(2,1)} async-done(((bf16[384,2304]{1,0:T(8,128)(2,1)}), bf16[96,2304]{1,0:T(8,128)(2,1)}) %reduce-scatter.29.cloned.1.call-update) | async-done | bytes 442384 | tf_op jit(solution)/shard_map/reduce_scatter | solution.py:266
  536.1 15.3 %all-reduce.20 = (bf16[768]{0:T(1024)(128)(2,1)S(1)}, bf16[768]{0:T(1024)(128)(2,1)S(1)}, bf16[384]{0:T(512)(128)(2,1)S(1)}, bf16[384]{0:T(512)(128)(2,1)S(1)}, ...) all-reduce(bf16[768]{0:T(1024)(128)(2,1)S(1)} %copy-done.118, ...), channel_id=25, replica_groups=mesh['shard'=4,'rep'=8] {'shard'}, use_global_device_ids=true, to_apply=%region_42.43.clone | all-reduce | flops 10752 | bytes 43008
  552.3 27.0 %all-reduce.18 = (bf16[1,192]{1,0:T(2,128)(2,1)S(1)}, bf16[1,192]{1,0:T(2,128)(2,1)S(1)}, bf16[1,96]{1,0:T(2,128)(2,1)S(1)}, bf16[1,96]{1,0:T(2,128)(2,1)S(1)}, ...) all-reduce(bf16[1,192]{1,0:T(2,128)(2,1)S(1)} %stack.145, ...), channel_id=1, replica_groups=mesh['shard'=4,'rep'=8] {'rep'}, use_global_device_ids=true, to_apply=%region_43.44 | all-reduce | flops 2688 | bytes 10752 | tf_op jit(solution)/shard_map/psum | solution.py:275
  582.8 29.2 %all-reduce.24.cloned.1.call-done = (bf16[1,96,1152]{2,1,0:T(8,128)(2,1)}, bf16[1,96,1152]{2,1,0:T(8,128)(2,1)}, bf16[1,96,384]{2,1,0:T(8,128)(2,1)}, bf16[1,96,...) async-done(((bf16[1,96,1152]{2,1,0:T(8,128)(2,1)}, ...) | async-done | bytes 2654224 | tf_op jit(solution)/shard_map/psum | solution.py:274
  (511 shorter events, 110.1 us)
Async XLA Ops:
  7.2 99.5 %all-gather.27.cloned.1.call-start = ((), (), s32[]{:S(2)}) async-start(), calls=%async_computation.20 | async-start | bytes 2211840 | tf_op jit(solution)/shard_map/all_gather | solution.py:214
  9.4 99.4 %all-gather.33.cloned.1.call-start = ((), (), s32[]{:S(2)}) async-start(), calls=%async_computation.23 | async-start | bytes 2211840 | tf_op jit(solution)/shard_map/all_gather | solution.py:214
  10.2 110.0 %all-gather.29.cloned.1.call-start = ((), (), s32[]{:S(2)}) async-start(), calls=%async_computation.21 | async-start | bytes 1474560 | tf_op jit(solution)/shard_map/all_gather | solution.py:210
  11.2 138.4 %all-gather.31.cloned.1.call-start = ((), (), s32[]{:S(2)}) async-start(), calls=%async_computation.22 | async-start | bytes 1474560 | tf_op jit(solution)/shard_map/all_gather | solution.py:212
  12.2 166.9 %all-gather.35.cloned.1.call-start = ((), (), s32[]{:S(2)}) async-start(), calls=%async_computation.24 | async-start | bytes 1474560 | tf_op jit(solution)/shard_map/all_gather | solution.py:210
  12.7 196.3 %all-gather.37.cloned.1.call-start = ((), (), s32[]{:S(2)}) async-start(), calls=%async_computation.25 | async-start | bytes 1474560 | tf_op jit(solution)/shard_map/all_gather | solution.py:212
  13.3 262.2 %reduce-scatter.17.cloned.1.call-start = ((), (), s32[]{:S(2)}) async-start(), calls=%async_computation.13 | async-start | bytes 368640 | tf_op jit(solution)/shard_map/reduce_scatter | solution.py:248
  226.6 51.4 %reduce-scatter.15.cloned.1.call-start = ((), (), s32[]{:S(2)}) async-start(), calls=%async_computation.12 | async-start | bytes 368640 | tf_op jit(solution)/shard_map/reduce_scatter | solution.py:248
  238.1 70.2 %reduce-scatter.13.cloned.1.call-start = ((), (), s32[]{:S(2)}) async-start(), calls=%async_computation.11 | async-start | bytes 1105920 | tf_op jit(solution)/shard_map/reduce_scatter | solution.py:242
  240.9 97.0 %reduce-scatter.11.cloned.1.call-start = ((), (), s32[]{:S(2)}) async-start(), calls=%async_computation.10 | async-start | bytes 1105920 | tf_op jit(solution)/shard_map/reduce_scatter | solution.py:242
  246.8 122.5 %reduce-scatter.25.cloned.1.call-start = ((), (), s32[]{:S(2)}) async-start(), calls=%async_computation.17 | async-start | bytes 1474560 | tf_op jit(solution)/shard_map/reduce_scatter | solution.py:260
  250.2 151.0 %reduce-scatter.21.cloned.1.call-start = ((), (), s32[]{:S(2)}) async-start(), calls=%async_computation.15 | async-start | bytes 1474560 | tf_op jit(solution)/shard_map/reduce_scatter | solution.py:254
  253.0 179.7 %reduce-scatter.23.cloned.1.call-start = ((), (), s32[]{:S(2)}) async-start(), calls=%async_computation.16 | async-start | bytes 1474560 | tf_op jit(solution)/shard_map/reduce_scatter | solution.py:260
  256.4 208.2 %reduce-scatter.19.cloned.1.call-start = ((), (), s32[]{:S(2)}) async-start(), calls=%async_computation.14 | async-start | bytes 1474560 | tf_op jit(solution)/shard_map/reduce_scatter | solution.py:254
  259.3 241.3 %reduce-scatter.27.cloned.1.call-start = ((), (), s32[]{:S(2)}) async-start(), calls=%async_computation.18 | async-start | bytes 2211840 | tf_op jit(solution)/shard_map/reduce_scatter | solution.py:266
  267.3 268.7 %reduce-scatter.29.cloned.1.call-start = ((), (), s32[]{:S(2)}) async-start(), calls=%async_computation.19 | async-start | bytes 2211840 | tf_op jit(solution)/shard_map/reduce_scatter | solution.py:266
  267.9 344.1 %all-reduce.24.cloned.1.call-start = ((), (), s32[]{:S(2)}) async-start(), calls=%async_computation.26 | async-start | bytes 5308416 | tf_op jit(solution)/shard_map/psum | solution.py:274
  275.4 260.6 %copy-start.118 = (bf16[768]{0:T(1024)(128)(2,1)S(1)}, bf16[768]{0:T(1024)(128)(2,1)}, u32[]{:S(2)}) copy-start(bf16[768]{0:T(1024)(128)(2,1)} %pad_maximum_fusion.7) | copy-start | bytes 4612
  275.4 260.6 %copy-start.123 = (bf16[384]{0:T(512)(128)(2,1)S(1)}, bf16[384]{0:T(512)(128)(2,1)}, u32[]{:S(2)}) copy-start(bf16[384]{0:T(512)(128)(2,1)} %get-tuple-element.93) | copy-start | bytes 2308
  275.4 260.6 %copy-start.124 = (bf16[384]{0:T(512)(128)(2,1)S(1)}, bf16[384]{0:T(512)(128)(2,1)}, u32[]{:S(2)}) copy-start(bf16[384]{0:T(512)(128)(2,1)} %get-tuple-element.122) | copy-start | bytes 2308
  275.5 260.6 %copy-start.125 = (bf16[384]{0:T(512)(128)(2,1)S(1)}, bf16[384]{0:T(512)(128)(2,1)}, u32[]{:S(2)}) copy-start(bf16[384]{0:T(512)(128)(2,1)} %get-tuple-element.87) | copy-start | bytes 2308
  275.5 276.5 %copy-start.119 = (f32[384]{0:T(512)S(1)}, f32[384]{0:T(512)}, u32[]{:S(2)}) copy-start(f32[384]{0:T(512)} %fusion.53) | copy-start | bytes 4612
  275.5 306.7 %copy-start.82 = (bf16[1,384]{1,0:T(2,128)(2,1)S(1)}, bf16[1,384]{1,0:T(2,128)(2,1)}, u32[]{:S(2)}) copy-start(bf16[1,384]{1,0:T(2,128)(2,1)} %param.14) | copy-start | bytes 2308
  275.5 306.7 %copy-start.84 = (f32[1,384]{1,0:T(1,128)S(1)}, f32[1,384]{1,0:T(1,128)}, u32[]{:S(2)}) copy-start(f32[1,384]{1,0:T(1,128)} %copy-done.83) | copy-start | bytes 4612
  (138 other events, 1704.1 us)
Sparse Core Ops, SparseCore 0:
  10.4 36.0 all-gather.26
  49.0 39.2 all-gather.32
  90.7 29.4 all-gather.28
  121.8 27.7 all-gather.30
  151.3 27.7 all-gather.34
  181.3 27.7 all-gather.36
  226.7 24.2 reduce-scatter.16
  253.7 24.2 reduce-scatter.14
  281.5 26.7 reduce-scatter.12
  311.1 26.6 reduce-scatter.10
  340.8 28.5 reduce-scatter.24
  372.7 28.5 reduce-scatter.20
  404.1 28.5 reduce-scatter.22
  436.1 28.5 reduce-scatter.18
  468.1 32.4 reduce-scatter.26
  503.5 32.4 reduce-scatter.28
  539.1 72.8 all-reduce.23
where the time goes:
time: 627 us; the launch traced here: 626 us
  waiting for transfers between devices  367 us (59%)
  blocking collectives  126 us (20%)
  matrix products  59.6 us (10%)
  other arithmetic  31.8 us (5%)
  local copies, waits for them, and re-layouts  20.1 us (3%)
  between operations  20 us (3%)
    reduce_scatter x2, waiting for transfers between devices, shards(): lax.psum_scatter(grads[8].astype(jnp.bfloat16), 'shard', scatter_dimensio...  71.4 us
    reduce_scatter x2, waiting for transfers between devices, shards(): lax.psum_scatter(grads[4].astype(jnp.bfloat16), 'shard', scatter_dimensio...  63.8 us
    reduce_scatter x2, waiting for transfers between devices, shards(): lax.psum_scatter(grads[6].astype(jnp.bfloat16), 'shard', scatter_dimensio...  63 us
    reduce_scatter x2, waiting for transfers between devices, shards(): lax.psum_scatter(grads[0].astype(jnp.bfloat16), 'shard', scatter_dimensio...  59.8 us
    all_gather x2, waiting for transfers between devices, shards(): lax.all_gather(w_fc2[layer_number], 'shard', axis=0, tiled=True)  53.2 us
    unnamed x2, blocking collectives  31.1 us
    psum x1, waiting for transfers between devices, shards(): lax.psum(owner_rows[0].astype(jnp.bfloat16), 'rep').astype(jnp.float32)  29.2 us
    all_gather x2, blocking collectives, shards(): lax.all_gather(w_qkv[layer_number], 'shard', axis=0, tiled=True)  28.9 us
  transfers between devices with their start and end apart: 17, of which 14 were waited for; matrix products, arithmetic and copies ran while one was open for 13% of the time, Pallas kernels for 0%

commit v1 on v0

--- a/solution.py
+++ b/solution.py
@@ -2,6 +2,7 @@
 import jax.numpy as jnp
 from jax import lax
 from jax.sharding import PartitionSpec as P
+from jax.lax import all_gather
 
 HEADS = 6
 
@@ -272,7 +273,9 @@
         )
         owner_rows = (
             lax.psum(owner_rows[0].astype(jnp.bfloat16), "rep").astype(jnp.float32),
-            lax.psum(owner_rows[1].astype(jnp.bfloat16), "rep").astype(jnp.float32),
+            jnp.sum(all_gather(owner_rows[1].astype(jnp.bfloat16), axis_name="rep"), axis=0).astype(
+                jnp.float32
+            ),
             lax.psum(owner_rows[2].astype(jnp.bfloat16), "rep").astype(jnp.float32),
             lax.psum(owner_rows[3].astype(jnp.bfloat16), "rep").astype(jnp.float32),
             lax.psum(owner_rows[4].astype(jnp.bfloat16), "rep").astype(jnp.float32),

time: 627 us -> 627 us (level)
  waiting for transfers between devices: 367 us -> 345 us
  local copies, waits for them, and re-layouts: 20.1 us -> 38.8 us
    unnamed x2 -> x3, blocking collectives: 31.1 us -> 62.6 us
    psum x1 -> x0, blocking collectives: 27 us -> none  [shards(): lax.psum(owner_rows[1].astype(jnp.bfloat16), 'rep').astype(jnp.float32)]
    reduce_scatter x2, waiting for transfers between devices: 59.8 us -> 47.7 us  [shards(): lax.psum_scatter(grads[0].astype(jnp.bfloat16), 'shard', scatter_dimensio...]
    psum x1, waiting for transfers between devices: 29.2 us -> 20.9 us  [shards(): lax.psum(owner_rows[0].astype(jnp.bfloat16), 'rep').astype(jnp.float32)]
    unnamed x325 -> x352, local copies, waits for them, and re-layouts: 9.73 us -> 17.9 us
  transfers between devices with their start and end apart: 17 -> 17, of which waited for: 14 -> 13; matrix products, arithmetic and copies ran while one was open for 13% -> 16% of each run, Pallas kernels for 0% -> 0%
where the time goes in v1:
time: 627 us; the launch traced here: 626 us
  waiting for transfers between devices  345 us (55%)
  blocking collectives  130 us (21%)
  matrix products  59.8 us (10%)
  local copies, waits for them, and re-layouts  38.8 us (6%)
  other arithmetic  30 us (5%)
  between operations  21.2 us (3%)
    reduce_scatter x2, waiting for transfers between devices, shards(): lax.psum_scatter(grads[8].astype(jnp.bfloat16), 'shard', scatter_dimensio...  71.3 us
    reduce_scatter x2, waiting for transfers between devices, shards(): lax.psum_scatter(grads[4].astype(jnp.bfloat16), 'shard', scatter_dimensio...  63.8 us
    reduce_scatter x2, waiting for transfers between devices, shards(): lax.psum_scatter(grads[6].astype(jnp.bfloat16), 'shard', scatter_dimensio...  63 us
    unnamed x3, blocking collectives  62.6 us
    all_gather x2, waiting for transfers between devices, shards(): lax.all_gather(w_fc2[layer_number], 'shard', axis=0, tiled=True)  53.2 us
    reduce_scatter x2, waiting for transfers between devices, shards(): lax.psum_scatter(grads[0].astype(jnp.bfloat16), 'shard', scatter_dimensio...  47.7 us
    all_gather x2, blocking collectives, shards(): lax.all_gather(w_qkv[layer_number], 'shard', axis=0, tiled=True)  28.8 us
    all_gather x2, waiting for transfers between devices, shards(): lax.all_gather(w_fc1[layer_number], 'shard', axis=0, tiled=True)  22 us
  transfers between devices with their start and end apart: 17, of which 13 were waited for; matrix products, arithmetic and copies ran while one was open for 16% of the time, Pallas kernels for 0%

profile of v1, /device:TPU:0, one launch (start us, length us, event | category | flops | bytes accessed | tf_op | source)
XLA Modules:
  0.0 625.6 jit_solution(659307407894853339)
XLA Ops:
  17.1 9.5 %all-gather.17 = bf16[1,1536]{1,0:T(2,128)(2,1)S(1)} all-gather(bf16[1,384]{1,0:T(2,128)(2,1)S(1)} %get-tuple-element.131), channel_id=19, replica_groups=mesh['shard'=4,'rep'=8] {'shard'}, dimensions={1}, use_global_device_ids=true | all-gather | bytes 3840 | tf_op jit(solution)/shard_map/all_gather | solution.py:212
  27.3 8.0 %all-gather.7 = bf16[1,1536]{1,0:T(2,128)(2,1)S(1)} all-gather(bf16[1,384]{1,0:T(2,128)(2,1)S(1)} %get-tuple-element.132), channel_id=9, replica_groups=mesh['shard'=4,'rep'=8] {'shard'}, dimensions={1}, use_global_device_ids=true | all-gather | bytes 3840 | tf_op jit(solution)/shard_map/all_gather | solution.py:212
  37.6 15.8 %all-reduce.23 = (bf16[2304]{0:T(1024)(128)(2,1)S(1)}, bf16[768]{0:T(1024)(128)(2,1)S(1)}, bf16[384]{0:T(512)(128)(2,1)S(1)}, bf16[384]{0:T(512)(128)(2,1)S(1)},...) all-reduce(bf16[2304]{0:T(1024)(128)(2,1)S(1)} %dynamic-update-slic, ...), channel_id=3, replica_groups=mesh['shard'=4,'rep'=8] {'shard'}, use_global_device_ids=true, to_apply=%add | all-reduce | flops 7680 | bytes 30720
  56.4 10.2 %all-gather.14 = bf16[1,384,384]{2,1,0:T(8,128)(2,1)} all-gather(bf16[1,96,384]{2,1,0:T(8,128)(2,1)S(1)} %get-tuple-element.123), channel_id=16, replica_groups=mesh['shard'=4,'rep'=8] {'shard'}, dimensions={1}, use_global_device_ids=true | all-gather | bytes 368640 | tf_op jit(solution)/shard_map/all_gather | solution.py:209
  66.6 11.1 %all-gather.4 = bf16[1,384,384]{2,1,0:T(8,128)(2,1)S(1)} all-gather(bf16[1,96,384]{2,1,0:T(8,128)(2,1)S(1)} %get-tuple-element.124), channel_id=6, replica_groups=mesh['shard'=4,'rep'=8] {'shard'}, dimensions={1}, use_global_device_ids=true | all-gather | bytes 368640 | tf_op jit(solution)/shard_map/all_gather | solution.py:209
  77.8 14.5 %all-gather.12 = bf16[1,384,1152]{2,1,0:T(8,128)(2,1)S(1)} all-gather(bf16[1,96,1152]{2,1,0:T(8,128)(2,1)S(1)} %get-tuple-element.114), channel_id=14, replica_groups=mesh['shard'=4,'rep'=8] {'shard'}, dimensions={1}, use_global_device_ids=true | all-gather | bytes 1105920 | tf_op jit(solution)/shard_map/all_gather | solution.py:207
  92.3 14.3 %all-gather.2 = bf16[1,384,1152]{2,1,0:T(8,128)(2,1)S(1)} all-gather(bf16[1,96,1152]{2,1,0:T(8,128)(2,1)S(1)} %get-tuple-element.115), channel_id=4, replica_groups=mesh['shard'=4,'rep'=8] {'shard'}, dimensions={1}, use_global_device_ids=true | all-gather | bytes 1105920 | tf_op jit(solution)/shard_map/all_gather | solution.py:207
  115.6 4.5 all-gather.31.cloned.1.call-done
  123.2 26.4 %all-gather.33.cloned.1.call-done = bf16[1,1536,384]{2,1,0:T(8,128)(2,1)} async-done(((bf16[1,384,384]{2,1,0:T(8,128)(2,1)}), bf16[1,1536,384]{2,1,0:T(8,128)(2,1)}) %all-gather.33.cloned.1.call-update) | async-done | bytes 1179664 | tf_op jit(solution)/shard_map/all_gather | solution.py:213
  161.5 17.5 %all-gather.37.cloned.1.call-done = bf16[1,384,1536]{2,1,0:T(8,128)(2,1)} async-done(((bf16[1,96,1536]{2,1,0:T(8,128)(2,1)}), bf16[1,384,1536]{2,1,0:T(8,128)(2,1)}) %all-gather.37.cloned.1.call-update) | async-done | bytes 1179664 | tf_op jit(solution)/shard_map/all_gather | solution.py:211
  182.2 26.9 %all-gather.39.cloned.1.call-done = bf16[1,1536,384]{2,1,0:T(8,128)(2,1)} async-done(((bf16[1,384,384]{2,1,0:T(8,128)(2,1)}), bf16[1,1536,384]{2,1,0:T(8,128)(2,1)}) %all-gather.39.cloned.1.call-update) | async-done | bytes 1179664 | tf_op jit(solution)/shard_map/all_gather | solution.py:213
  209.0 4.0 fusion.165
  246.8 3.3 convolution_convert_fusion.2
  272.5 16.1 %all-reduce.22 = (bf16[768]{0:T(1024)(128)(2,1)}, bf16[768]{0:T(1024)(128)(2,1)}, bf16[384]{0:T(512)(128)(2,1)S(1)}, bf16[384]{0:T(512)(128)(2,1)S(1)}, bf16[153...) all-reduce(bf16[768]{0:T(1024)(128)(2,1)S(1)} %pad_maximum_fusion.7, ...), channel_id=27, replica_groups=mesh['shard'=4,'rep'=8] {'shard'}, use_global_device_ids=true, to_apply=%region_42.43.clone | all-reduce | flops 10752 | bytes 43008
  290.0 18.2 %reduce-scatter.13.cloned.1.call-done = bf16[96,1152]{1,0:T(8,128)(2,1)} async-done(((bf16[384,1152]{1,0:T(8,128)(2,1)}), bf16[96,1152]{1,0:T(8,128)(2,1)}) %reduce-scatter.13.cloned.1.call-update) | async-done | bytes 221200 | tf_op jit(solution)/shard_map/reduce_scatter | solution.py:243
  308.2 29.5 %reduce-scatter.11.cloned.1.call-done = bf16[96,1152]{1,0:T(8,128)(2,1)} async-done(((bf16[384,1152]{1,0:T(8,128)(2,1)}), bf16[96,1152]{1,0:T(8,128)(2,1)}) %reduce-scatter.11.cloned.1.call-update) | async-done | bytes 221200 | tf_op jit(solution)/shard_map/reduce_scatter | solution.py:243
  337.7 31.5 %reduce-scatter.25.cloned.1.call-done = bf16[384,384]{1,0:T(8,128)(2,1)} async-done(((bf16[1536,384]{1,0:T(8,128)(2,1)}), bf16[384,384]{1,0:T(8,128)(2,1)}) %reduce-scatter.25.cloned.1.call-update) | async-done | bytes 294928 | tf_op jit(solution)/shard_map/reduce_scatter | solution.py:261
  369.2 31.9 %reduce-scatter.21.cloned.1.call-done = bf16[96,1536]{1,0:T(8,128)(2,1)} async-done(((bf16[384,1536]{1,0:T(8,128)(2,1)}), bf16[96,1536]{1,0:T(8,128)(2,1)}) %reduce-scatter.21.cloned.1.call-update) | async-done | bytes 294928 | tf_op jit(solution)/shard_map/reduce_scatter | solution.py:255
  401.1 31.5 %reduce-scatter.23.cloned.1.call-done = bf16[384,384]{1,0:T(8,128)(2,1)} async-done(((bf16[1536,384]{1,0:T(8,128)(2,1)}), bf16[384,384]{1,0:T(8,128)(2,1)}) %reduce-scatter.23.cloned.1.call-update) | async-done | bytes 294928 | tf_op jit(solution)/shard_map/reduce_scatter | solution.py:261
  432.6 31.9 %reduce-scatter.19.cloned.1.call-done = bf16[96,1536]{1,0:T(8,128)(2,1)} async-done(((bf16[384,1536]{1,0:T(8,128)(2,1)}), bf16[96,1536]{1,0:T(8,128)(2,1)}) %reduce-scatter.19.cloned.1.call-update) | async-done | bytes 294928 | tf_op jit(solution)/shard_map/reduce_scatter | solution.py:255
  464.5 36.0 %reduce-scatter.27.cloned.1.call-done = bf16[96,2304]{1,0:T(8,128)(2,1)} async-done(((bf16[384,2304]{1,0:T(8,128)(2,1)}), bf16[96,2304]{1,0:T(8,128)(2,1)}) %reduce-scatter.27.cloned.1.call-update) | async-done | bytes 442384 | tf_op jit(solution)/shard_map/reduce_scatter | solution.py:267
  500.4 35.4 %reduce-scatter.29.cloned.1.call-done = bf16[96,2304]{1,0:T(8,128)(2,1)} async-done(((bf16[384,2304]{1,0:T(8,128)(2,1)}), bf16[96,2304]{1,0:T(8,128)(2,1)}) %reduce-scatter.29.cloned.1.call-update) | async-done | bytes 442384 | tf_op jit(solution)/shard_map/reduce_scatter | solution.py:267
  550.0 30.7 %all-reduce.20 = (bf16[1536]{0:T(1024)(128)(2,1)}, bf16[1536]{0:T(1024)(128)(2,1)}, bf16[1,96]{1,0:T(2,128)(2,1)}, bf16[1,96]{1,0:T(2,128)(2,1)}, bf16[1,384]{1,...) all-reduce(bf16[1536]{0:T(1024)(128)(2,1)S(1)} %dynamic-update-slic, ...), channel_id=23, replica_groups=mesh['shard'=4,'rep'=8] {'rep'}, use_global_device_ids=true, to_apply=%add.9 | all-reduce | flops 5376 | bytes 21504
  590.8 20.9 %all-reduce.26.cloned.1.call-done = (bf16[1,96,1152]{2,1,0:T(8,128)(2,1)}, bf16[1,96,1152]{2,1,0:T(8,128)(2,1)}, bf16[1,96,384]{2,1,0:T(8,128)(2,1)}, bf16[1,96,...) async-done(((bf16[1,96,1152]{2,1,0:T(8,128)(2,1)}, ...) | async-done | bytes 2654224 | tf_op jit(solution)/shard_map/psum | solution.py:275
  (542 shorter events, 124.8 us)
Async XLA Ops:
  7.2 99.4 %all-gather.29.cloned.1.call-start = ((), (), s32[]{:S(2)}) async-start(), calls=%async_computation.20 | async-start | bytes 2211840 | tf_op jit(solution)/shard_map/all_gather | solution.py:215
  9.4 99.4 %all-gather.35.cloned.1.call-start = ((), (), s32[]{:S(2)}) async-start(), calls=%async_computation.23 | async-start | bytes 2211840 | tf_op jit(solution)/shard_map/all_gather | solution.py:215
  10.2 109.9 %all-gather.31.cloned.1.call-start = ((), (), s32[]{:S(2)}) async-start(), calls=%async_computation.21 | async-start | bytes 1474560 | tf_op jit(solution)/shard_map/all_gather | solution.py:211
  11.2 138.4 %all-gather.33.cloned.1.call-start = ((), (), s32[]{:S(2)}) async-start(), calls=%async_computation.22 | async-start | bytes 1474560 | tf_op jit(solution)/shard_map/all_gather | solution.py:213
  12.1 65.6 %copy-start.55 = (bf16[2,96,1152]{2,1,0:T(8,128)(2,1)S(1)}, bf16[2,96,1152]{2,1,0:T(8,128)(2,1)}, u32[]{:S(2)}) copy-start(bf16[2,96,1152]{2,1,0:T(8,128)(2,1)} %param.16) | copy-start | bytes 1327108
  12.2 166.8 %all-gather.37.cloned.1.call-start = ((), (), s32[]{:S(2)}) async-start(), calls=%async_computation.24 | async-start | bytes 1474560 | tf_op jit(solution)/shard_map/all_gather | solution.py:211
  12.8 196.3 %all-gather.39.cloned.1.call-start = ((), (), s32[]{:S(2)}) async-start(), calls=%async_computation.25 | async-start | bytes 1474560 | tf_op jit(solution)/shard_map/all_gather | solution.py:213
  13.3 276.6 %reduce-scatter.17.cloned.1.call-start = ((), (), s32[]{:S(2)}) async-start(), calls=%async_computation.13 | async-start | bytes 368640 | tf_op jit(solution)/shard_map/reduce_scatter | solution.py:249
  16.1 95.8 %copy-start.95 = (f32[256]{0:T(256)}, f32[256]{0:T(256)S(1)}, u32[]{:S(2)}) copy-start(f32[256]{0:T(256)S(1)} %broadcast_multiply_fusion.11) | copy-start | bytes 3076
  16.4 95.6 %copy-start.106 = (f32[256]{0:T(256)}, f32[256]{0:T(256)S(1)}, u32[]{:S(2)}) copy-start(f32[256]{0:T(256)S(1)} %add_rsqrt_fusion.3) | copy-start | bytes 3076
  17.1 91.7 %copy-start.86 = (f32[1,384]{1,0:T(1,128)}, f32[1,384]{1,0:T(1,128)S(1)}, u32[]{:S(2)}) copy-start(f32[1,384]{1,0:T(1,128)S(1)} %get-tuple-element.97) | copy-start | bytes 4612
  92.3 60.7 %copy-start.13 = (bf16[1,384,1152]{2,1,0:T(8,128)(2,1)}, bf16[1,384,1152]{2,1,0:T(8,128)(2,1)S(1)}, u32[]{:S(2)}) copy-start(bf16[1,384,1152]{2,1,0:T(8,128)(2,1)S(1)} %all-gather.12) | copy-start | bytes 2654212
  226.6 63.4 %reduce-scatter.15.cloned.1.call-start = ((), (), s32[]{:S(2)}) async-start(), calls=%async_computation.12 | async-start | bytes 368640 | tf_op jit(solution)/shard_map/reduce_scatter | solution.py:249
  238.1 70.1 %reduce-scatter.13.cloned.1.call-start = ((), (), s32[]{:S(2)}) async-start(), calls=%async_computation.11 | async-start | bytes 1105920 | tf_op jit(solution)/shard_map/reduce_scatter | solution.py:243
  240.8 96.9 %reduce-scatter.11.cloned.1.call-start = ((), (), s32[]{:S(2)}) async-start(), calls=%async_computation.10 | async-start | bytes 1105920 | tf_op jit(solution)/shard_map/reduce_scatter | solution.py:243
  246.7 122.4 %reduce-scatter.25.cloned.1.call-start = ((), (), s32[]{:S(2)}) async-start(), calls=%async_computation.17 | async-start | bytes 1474560 | tf_op jit(solution)/shard_map/reduce_scatter | solution.py:261
  250.2 150.9 %reduce-scatter.21.cloned.1.call-start = ((), (), s32[]{:S(2)}) async-start(), calls=%async_computation.15 | async-start | bytes 1474560 | tf_op jit(solution)/shard_map/reduce_scatter | solution.py:255
  252.9 179.6 %reduce-scatter.23.cloned.1.call-start = ((), (), s32[]{:S(2)}) async-start(), calls=%async_computation.16 | async-start | bytes 1474560 | tf_op jit(solution)/shard_map/reduce_scatter | solution.py:261
  256.3 208.2 %reduce-scatter.19.cloned.1.call-start = ((), (), s32[]{:S(2)}) async-start(), calls=%async_computation.14 | async-start | bytes 1474560 | tf_op jit(solution)/shard_map/reduce_scatter | solution.py:255
  259.3 241.2 %reduce-scatter.27.cloned.1.call-start = ((), (), s32[]{:S(2)}) async-start(), calls=%async_computation.18 | async-start | bytes 2211840 | tf_op jit(solution)/shard_map/reduce_scatter | solution.py:267
  267.2 268.6 %reduce-scatter.29.cloned.1.call-start = ((), (), s32[]{:S(2)}) async-start(), calls=%async_computation.19 | async-start | bytes 2211840 | tf_op jit(solution)/shard_map/reduce_scatter | solution.py:267
  267.8 343.9 %all-reduce.26.cloned.1.call-start = ((), (), s32[]{:S(2)}) async-start(), calls=%async_computation.26 | async-start | bytes 5308416 | tf_op jit(solution)/shard_map/psum | solution.py:275
  272.4 312.7 %copy-start.4 = (bf16[1,384,2304]{2,1,0:T(8,128)(2,1)S(1)}, bf16[1,384,2304]{2,1,0:T(8,128)(2,1)}, u32[]{:S(2)}) copy-start(bf16[1,384,2304]{2,1,0:T(8,128)(2,1)} %all-gather.35.cloned.1.call-done) | copy-start | bytes 5308420
  535.8 50.7 %copy-start.3 = (bf16[1,384,2304]{2,1,0:T(8,128)(2,1)S(1)}, bf16[1,384,2304]{2,1,0:T(8,128)(2,1)}, u32[]{:S(2)}) copy-start(bf16[1,384,2304]{2,1,0:T(8,128)(2,1)} %all-gather.29.cloned.1.call-done) | copy-start | bytes 5308420
  (149 other events, 616.2 us)
Sparse Core Ops, SparseCore 0:
  10.4 36.0 all-gather.28
  49.0 39.2 all-gather.34
  90.7 29.3 all-gather.30
  121.8 27.7 all-gather.32
  151.2 27.7 all-gather.36
  181.3 27.7 all-gather.38
  226.7 24.1 reduce-scatter.16
  253.7 24.2 reduce-scatter.14
  281.5 26.6 reduce-scatter.12
  311.0 26.6 reduce-scatter.10
  340.6 28.5 reduce-scatter.24
  372.5 28.5 reduce-scatter.20
  404.0 28.5 reduce-scatter.22
  435.9 28.5 reduce-scatter.18
  467.9 32.4 reduce-scatter.26
  503.3 32.4 reduce-scatter.28
  538.9 72.7 all-reduce.25
